TPU v7x, 512 devices: a whole 4x8x8 slice. The times are simulated.
512 devices in a mesh: hosp: 32 (over z_hi, y, core), seq: 16 (over z_lo, x).
Axes of the slice: x: 4, y: 8, z: 8 (z_hi: 2, z_lo: 4; z = z_hi * 4 + z_lo), core: 2. Of those that a mesh axis runs over, the one named last changes fastest.
Arguments:
- frames: bfloat16 [32, 8192, 512], P('hosp', 'seq'), may hold values from -6 to 6
- cotangent: bfloat16 [32, 8192, 512], P('hosp', 'seq'), may hold values from -6 to 6
- first_filter: bfloat16 [3, 512, 512], replicated, may hold values from -0.15625 to 0.15625
- second_filter: bfloat16 [3, 512, 512], replicated, may hold values from -0.15625 to 0.15625
Outputs:
- input_gradient: bfloat16 [32, 8192, 512], P('hosp', 'seq')
- grad_one: float32 [512, 3, 512], P('seq', None, 'hosp')
- grad_two: float32 [512, 3, 512], P('seq', None, 'hosp')
All inputs are finite; a program needn't handle non-finite values.
Results may differ from a plain program's by a relative error of at most 0.017.
Values may be sent and summed in bfloat16 or wider, within the bound.
A program may use at most 64 MiB of HBM per device.

v0:
```python
import math

import jax
import jax.numpy as jnp
from jax import lax
from jax.sharding import PartitionSpec as P

FIRST_DILATION = 512
SECOND_DILATION = 1024


def passed_along(block, axis, distance):
    devices = range(lax.axis_size(axis))
    route = [(i - distance, i) for i in devices if i - distance in devices]
    return lax.ppermute(block, axis, route)


def silu_grad(value):
    sigma = jax.nn.sigmoid(value)
    return sigma * (1.0 + value * (1.0 - sigma))


def relay_step(field):
    return passed_along(field, "seq", 1)


def fetch_past(field, hops):
    current = field
    near = field
    for step in range(2 * hops):
        current = relay_step(current)
        if step + 1 == hops:
            near = current
    return (near, current)


def delta_step(field, hops):
    return passed_along(field, "seq", -hops)


def back_grad(base, delta, filters, hops):
    stack = jnp.stack([delta, delta_step(delta, hops), delta_step(delta, 2 * hops)], axis=1)
    return base + jnp.einsum("tko,kio->ti", stack, filters, preferred_element_type=jnp.float32)


def reduce_filters(stack, delta, scale):
    shares = lax.psum_scatter(
        jnp.einsum("tki,to->iko", stack, delta, preferred_element_type=jnp.float32).astype(
            jnp.bfloat16
        ),
        "seq",
        scatter_dimension=0,
        tiled=True,
    ).astype(jnp.float32)
    held = lax.psum_scatter(shares, "hosp", scatter_dimension=2, tiled=True)
    return held * scale


def per_device(frames, cotangent, first_filter, second_filter):
    inputs = frames[0]
    upstream = cotangent[0]
    frame_rows, channels = inputs.shape
    first_hops = FIRST_DILATION // frame_rows
    second_hops = SECOND_DILATION // frame_rows
    near, far = fetch_past(inputs, first_hops)
    first_stack = jnp.stack([inputs, near, far], axis=1)
    pre_one = jnp.dot(
        first_stack.reshape(frame_rows, 3 * channels),
        first_filter.reshape(3 * channels, channels),
        preferred_element_type=jnp.float32,
    )
    hidden_state = (inputs.astype(jnp.float32) + jax.nn.silu(pre_one)).astype(jnp.bfloat16)
    near, far = fetch_past(hidden_state, second_hops)
    second_stack = jnp.stack([hidden_state, near, far], axis=1)
    pre_two = jnp.dot(
        second_stack.reshape(frame_rows, 3 * channels),
        second_filter.reshape(3 * channels, channels),
        preferred_element_type=jnp.float32,
    )
    upstream_f = upstream.astype(jnp.float32)
    second_delta = (upstream_f * silu_grad(pre_two)).astype(jnp.bfloat16)
    hidden_gradient = back_grad(upstream_f, second_delta, second_filter, second_hops)
    first_delta = (hidden_gradient * silu_grad(pre_one)).astype(jnp.bfloat16)
    input_gradient = back_grad(hidden_gradient, first_delta, first_filter, first_hops).astype(
        jnp.bfloat16
    )
    scale = 1.0 / math.sqrt(lax.axis_size("hosp") * frame_rows * lax.axis_size("seq"))
    grad_two = reduce_filters(second_stack, second_delta, scale)
    grad_one = reduce_filters(first_stack, first_delta, scale)
    return (input_gradient[None], grad_one, grad_two)


def solution(mesh):
    in_specs = (P("hosp", "seq", None), P("hosp", "seq", None), P(), P())
    out_specs = (P("hosp", "seq", None), P("seq", None, "hosp"), P("seq", None, "hosp"))
    return jax.shard_map(
        per_device, mesh=mesh, in_specs=in_specs, out_specs=out_specs, check_vma=False
    )
```

profile of v0, /device:TPU:6, one launch (start us, length us, event | category | flops | bytes accessed | tf_op | source)
XLA Modules:
  0.0 689.8 jit_solution(2679390986471024625)
XLA Ops:
  7.2 4.3 collective-permute-start
  11.6 11.6 %collective-permute-done = bf16[512,512]{1,0:T(8,128)(2,1)S(1)} collective-permute-done((bf16[512,512]{1,0:T(8,128)(2,1)}, bf16[512,512]{1,0:T(8,128)(2,1)S(1)}, u32[]{:S(2)}, u32[]{:S(2)}) %collective-permute-start) | collective-permute-done | bytes 524320 | tf_op jit(solution)/shard_map/ppermute | solution.py:15
  23.1 6.3 collective-permute-start.1
  29.4 10.3 %collective-permute-done.1 = bf16[512,512]{1,0:T(8,128)(2,1)S(1)} collective-permute-done((bf16[512,512]{1,0:T(8,128)(2,1)S(1)}, bf16[512,512]{1,0:T(8,128)(2,1)S(1)}, u32[]{:S(2)}, u32[]{:S(2)}) %collective-permute-start.1) | collective-permute-done | bytes 524320 | tf_op jit(solution)/shard_map/ppermute | solution.py:15
  39.7 3.9 add_convert_fusion
  43.7 6.5 collective-permute-start.2
  50.2 9.4 %collective-permute-done.2 = bf16[512,512]{1,0:T(8,128)(2,1)S(1)} collective-permute-done((bf16[512,512]{1,0:T(8,128)(2,1)S(1)}, bf16[512,512]{1,0:T(8,128)(2,1)S(1)}, u32[]{:S(2)}, u32[]{:S(2)}) %collective-permute-start.2) | collective-permute-done | bytes 524320 | tf_op jit(solution)/shard_map/ppermute | solution.py:15
  59.6 6.5 collective-permute-start.3
  66.1 8.6 %collective-permute-done.3 = bf16[512,512]{1,0:T(8,128)(2,1)S(1)} collective-permute-done((bf16[512,512]{1,0:T(8,128)(2,1)S(1)}, bf16[512,512]{1,0:T(8,128)(2,1)S(1)}, u32[]{:S(2)}, u32[]{:S(2)}) %collective-permute-start.3) | collective-permute-done | bytes 524320 | tf_op jit(solution)/shard_map/ppermute | solution.py:15
  74.7 6.5 collective-permute-start.4
  81.2 7.7 %collective-permute-done.4 = bf16[512,512]{1,0:T(8,128)(2,1)S(1)} collective-permute-done((bf16[512,512]{1,0:T(8,128)(2,1)S(1)}, bf16[512,512]{1,0:T(8,128)(2,1)S(1)}, u32[]{:S(2)}, u32[]{:S(2)}) %collective-permute-start.4) | collective-permute-done | bytes 524320 | tf_op jit(solution)/shard_map/ppermute | solution.py:15
  88.9 6.5 collective-permute-start.5
  95.4 6.9 collective-permute-done.5
  102.3 2.1 fusion.32
  107.6 2.1 fusion.13
  109.7 3.0 copy.28
  112.7 3.4 collective-permute-done.7
  116.1 11.0 %collective-permute-done.6 = bf16[512,512]{1,0:T(8,128)(2,1)} collective-permute-done((bf16[512,512]{1,0:T(8,128)(2,1)}, bf16[512,512]{1,0:T(8,128)(2,1)}, u32[]{:S(2)}, u32[]{:S(2)}) %collective-permute-start.6) | collective-permute-done | bytes 524320 | tf_op jit(solution)/shard_map/ppermute | solution.py:15
  127.1 4.3 multiply_convert_fusion
  133.5 3.1 copy.24
  140.5 4.9 collective-permute-start.8
  145.4 177.4 %all-reduce.11.cloned.1.call-done = (bf16[512,3,512]{2,1,0:T(4,128)(2,1)}, bf16[512,3,512]{2,1,0:T(4,128)(2,1)}) async-done(((bf16[512,3,512]{2,1,0:T(4,128)(2,1)}, bf16[512,3,512]{2,1,0:T(4,128)(2,1)}), (bf16[512,3,512]{2,1,0:T(4,128)(2,1)}, bf16[512,3,512]{2,1,0:T(4,128)(2,1)})) %all-reduce.11.cloned.1.call-update) | async-done | bytes 3145744
  328.6 3.5 fusion.29
  332.1 348.1 %all-reduce.9.cloned.1.call-done = (f32[32,3,512]{0,1,2:T(4,128)}, f32[32,3,512]{0,1,2:T(4,128)}) async-done(((f32[32,3,512]{0,1,2:T(4,128)}, f32[32,3,512]{0,1,2:T(4,128)}), (f32[32,3,512]{0,1,2:T(4,128)}, f32[32,3,512]{0,1,2:T(4,128)})) %all-reduce.9.cloned.1.call-update) | async-done | bytes 393232
  (37 shorter events, 16.4 us)
Async XLA Ops:
  7.2 95.2 %copy-start = (bf16[3,512,512]{2,1,0:T(8,128)(2,1)S(1)}, bf16[3,512,512]{2,1,0:T(8,128)(2,1)}, u32[]{:S(2)}) copy-start(bf16[3,512,512]{2,1,0:T(8,128)(2,1)} %param.7) | copy-start | bytes 4718596
  7.2 315.7 %all-reduce.11.cloned.1.call-start = ((), (), s32[]{:S(2)}) async-start(), calls=%async_computation.1 | async-start | bytes 8388608
  7.2 15.9 %collective-permute-start = (bf16[512,512]{1,0:T(8,128)(2,1)}, bf16[512,512]{1,0:T(8,128)(2,1)S(1)}, u32[]{:S(2)}, u32[]{:S(2)}) collective-permute-start(bf16[512,512]{1,0:T(8,128)(2,1)} %bitcast.54), channel_id=1, source_target_pairs={{0,1},{1,2},{2,3},{3,4},{4,5},{5,6},{6,7},{7,8},{8,9},{9,10},{10,1... | collective-permute-start | bytes 1572872 | tf_op jit(solution)/shard_map/ppermute | solution.py:15
  23.1 20.6 %copy-start.4 = (bf16[512,512]{1,0:T(8,128)(2,1)}, bf16[512,512]{1,0:T(8,128)(2,1)S(1)}, u32[]{:S(2)}) copy-start(bf16[512,512]{1,0:T(8,128)(2,1)S(1)} %collective-permute-done) | copy-start | bytes 1572868
  23.1 16.6 %collective-permute-start.1 = (bf16[512,512]{1,0:T(8,128)(2,1)S(1)}, bf16[512,512]{1,0:T(8,128)(2,1)S(1)}, u32[]{:S(2)}, u32[]{:S(2)}) collective-permute-start(bf16[512,512]{1,0:T(8,128)(2,1)S(1)} %collective-permute-done), channel_id=1, source_target_pairs={{0,1},{1,2},{2,3},{3,4},{4,5},{5,6},{6,7},{7,8},{8,9},{9,10},{10,1... | collective-permute-start | bytes 1572872 | tf_op jit(solution)/shard_map/ppermute | solution.py:15
  39.7 3.9 copy-start.6
  39.7 62.6 %copy-start.2 = (bf16[1,512,512]{2,1,0:T(8,128)(2,1)S(1)}, bf16[1,512,512]{2,1,0:T(8,128)(2,1)}, u32[]{:S(2)}) copy-start(bf16[1,512,512]{2,1,0:T(8,128)(2,1)} %param.5) | copy-start | bytes 1572868
  43.7 15.9 %collective-permute-start.2 = (bf16[512,512]{1,0:T(8,128)(2,1)S(1)}, bf16[512,512]{1,0:T(8,128)(2,1)S(1)}, u32[]{:S(2)}, u32[]{:S(2)}) collective-permute-start(bf16[512,512]{1,0:T(8,128)(2,1)S(1)} %get-tuple-element.16), channel_id=1, source_target_pairs={{0,1},{1,2},{2,3},{3,4},{4,5},{5,6},{6,7},{7,8},{8,9},{9,10},{10,1... | collective-permute-start | bytes 1572872 | tf_op jit(solution)/shard_map/ppermute | solution.py:15
  59.6 15.1 %collective-permute-start.3 = (bf16[512,512]{1,0:T(8,128)(2,1)S(1)}, bf16[512,512]{1,0:T(8,128)(2,1)S(1)}, u32[]{:S(2)}, u32[]{:S(2)}) collective-permute-start(bf16[512,512]{1,0:T(8,128)(2,1)S(1)} %collective-permute-done.2), channel_id=1, source_target_pairs={{0,1},{1,2},{2,3},{3,4},{4,5},{5,6},{6,7},{7,8},{8,9},{9,10},{10,1... | collective-permute-start | bytes 1572872 | tf_op jit(solution)/shard_map/ppermute | solution.py:15
  74.7 14.2 %collective-permute-start.4 = (bf16[512,512]{1,0:T(8,128)(2,1)S(1)}, bf16[512,512]{1,0:T(8,128)(2,1)S(1)}, u32[]{:S(2)}, u32[]{:S(2)}) collective-permute-start(bf16[512,512]{1,0:T(8,128)(2,1)S(1)} %collective-permute-done.3), channel_id=1, source_target_pairs={{0,1},{1,2},{2,3},{3,4},{4,5},{5,6},{6,7},{7,8},{8,9},{9,10},{10,1... | collective-permute-start | bytes 1572872 | tf_op jit(solution)/shard_map/ppermute | solution.py:15
  88.9 13.4 %collective-permute-start.5 = (bf16[512,512]{1,0:T(8,128)(2,1)S(1)}, bf16[512,512]{1,0:T(8,128)(2,1)S(1)}, u32[]{:S(2)}, u32[]{:S(2)}) collective-permute-start(bf16[512,512]{1,0:T(8,128)(2,1)S(1)} %collective-permute-done.4), channel_id=1, source_target_pairs={{0,1},{1,2},{2,3},{3,4},{4,5},{5,6},{6,7},{7,8},{8,9},{9,10},{10,1... | collective-permute-start | bytes 1572872 | tf_op jit(solution)/shard_map/ppermute | solution.py:15
  104.4 11.7 %collective-permute-start.7 = (bf16[512,512]{1,0:T(8,128)(2,1)}, bf16[512,512]{1,0:T(8,128)(2,1)}, u32[]{:S(2)}, u32[]{:S(2)}) collective-permute-start(bf16[512,512]{1,0:T(8,128)(2,1)} %fusion.32), channel_id=1, source_target_pairs={{4,0},{5,1},{6,2},{7,3},{8,4},{9,5},{10,6},{11,7},{12,8},{13,9},{1... | collective-permute-start | bytes 1572872 | tf_op jit(solution)/shard_map/ppermute | solution.py:15
  105.7 21.4 %collective-permute-start.6 = (bf16[512,512]{1,0:T(8,128)(2,1)}, bf16[512,512]{1,0:T(8,128)(2,1)}, u32[]{:S(2)}, u32[]{:S(2)}) collective-permute-start(bf16[512,512]{1,0:T(8,128)(2,1)} %fusion.32), channel_id=1, source_target_pairs={{2,0},{3,1},{4,2},{5,3},{6,4},{7,5},{8,6},{9,7},{10,8},{11,9},{12,... | collective-permute-start | bytes 1572872 | tf_op jit(solution)/shard_map/ppermute | solution.py:15
  127.1 4.3 copy-start.3
  127.1 4.3 copy-start.5
  127.1 4.3 copy-start.7
  136.6 543.6 %all-reduce.9.cloned.1.call-start = ((), (), s32[]{:S(2)}) async-start(), calls=%async_computation | async-start | bytes 4194304
  138.6 190.0 %collective-permute-start.9 = (bf16[512,512]{1,0:T(8,128)(2,1)}, bf16[512,512]{1,0:T(8,128)(2,1)}, u32[]{:S(2)}, u32[]{:S(2)}) collective-permute-start(bf16[512,512]{1,0:T(8,128)(2,1)} %get-tuple-element.18), channel_id=1, source_target_pairs={{2,0},{3,1},{4,2},{5,3},{6,4},{7,5},{8,6},{9,7},{10,8},{11,9},{12,... | collective-permute-start | bytes 1572872 | tf_op jit(solution)/shard_map/ppermute | solution.py:15
  140.5 188.1 %collective-permute-start.8 = (bf16[512,512]{1,0:T(8,128)(2,1)}, bf16[512,512]{1,0:T(8,128)(2,1)}, u32[]{:S(2)}, u32[]{:S(2)}) collective-permute-start(bf16[512,512]{1,0:T(8,128)(2,1)} %get-tuple-element.18), channel_id=1, source_target_pairs={{1,0},{2,1},{3,2},{4,3},{5,4},{6,5},{7,6},{8,7},{9,8},{10,9},{11,1... | collective-permute-start | bytes 1572872 | tf_op jit(solution)/shard_map/ppermute | solution.py:15
  325.3 3.3 copy-start.1
Sparse Core Ops, SparseCore 0:
  136.7 186.0 all-reduce.10
  326.8 353.4 all-reduce.8
where the time goes:
time: 692 us; the launch traced here: 690 us
  waiting for transfers between devices  595 us (86%)
  starting transfers between devices  46.6 us (7%)
  matrix products  18 us (3%)
  between operations  15.5 us (2%)
  local copies, waits for them, and re-layouts  13.6 us (2%)
    unnamed x4, waiting for transfers between devices  526 us
    ppermute x10, waiting for transfers between devices, passed_along(): return lax.ppermute(block, axis, route)  68.9 us
    ppermute x10, starting transfers between devices, passed_along(): return lax.ppermute(block, axis, route)  46.6 us
  transfers between devices with their start and end apart: 12, of which 10 were waited for; matrix products, arithmetic and copies ran while one was open for 2% of the time, Pallas kernels for 0%

commit v1 on v0

v1 whole, which is shorter than its diff:
```python
import math

import jax
import jax.numpy as jnp
from jax import lax
from jax.sharding import PartitionSpec as P

FIRST_DILATION = 512
SECOND_DILATION = 1024
BF = jnp.bfloat16
F32 = jnp.float32


def silu_grad(value):
    sigma = jax.nn.sigmoid(value)
    return sigma * (1.0 + value * (1.0 - sigma))


def regroup(block, n):
    rows, channels = block.shape
    parts = block.reshape(n, rows // n, channels)
    return lax.all_to_all(parts, "seq", 0, 0).reshape(rows, channels)


def past(v, s):
    return jnp.concatenate([jnp.zeros((s, v.shape[1]), v.dtype), v[: v.shape[0] - s]], axis=0)


def ahead(v, s):
    return jnp.concatenate([v[s:], jnp.zeros((s, v.shape[1]), v.dtype)], axis=0)


def dot(a, b):
    return jnp.dot(a, b, preferred_element_type=F32)


def conv(v, w, s):
    return dot(v, w[0]) + dot(past(v, s), w[1]) + dot(past(v, 2 * s), w[2])


def conv_back(d, w, s):
    total = None
    for k in range(3):
        term = lax.dot_general(
            d if k == 0 else ahead(d, k * s), w[k], (((1,), (1,)), ((), ())),
            preferred_element_type=F32,
        )
        total = term if total is None else total + term
    return total


def filter_share(v, delta, s, mine, n_seq, n_hosp):
    channels = v.shape[1]
    turned = dot(delta, mine).astype(BF)
    terms = jnp.stack(
        [
            lax.dot_general(
                v if k == 0 else past(v, k * s), turned, (((0,), (0,)), ((), ())),
                preferred_element_type=F32,
            )
            for k in range(3)
        ]
    )
    half = channels // 2
    swap = [(i, i ^ 1) for i in range(n_hosp)]
    other = lax.ppermute(terms[:, :, half:].astype(BF), "hosp", swap)
    pair = (terms[:, :, :half] + other.astype(F32)).astype(BF)
    depth = channels // n_seq
    pair = pair.reshape(3, n_seq, depth, half).transpose(1, 0, 2, 3)
    pair = lax.all_to_all(pair, "seq", 0, 0)
    return jnp.sum(pair.astype(F32), axis=0).astype(BF)


def per_device(frames, cotangent, first_filter, second_filter):
    n_seq = lax.axis_size("seq")
    n_hosp = lax.axis_size("hosp")
    rows, channels = frames.shape[1:]
    s1 = FIRST_DILATION // n_seq
    s2 = SECOND_DILATION // n_seq
    inputs = regroup(frames[0], n_seq)
    upstream = regroup(cotangent[0], n_seq).astype(F32)

    core = lax.axis_index("hosp") % 2
    width = channels // n_hosp
    half = channels // 2
    j = jnp.arange(channels)
    jj = j % half
    source = (jj // width) * (2 * width) + jnp.where(j < half, core, 1 - core) * width + jj % width
    mine = (jnp.arange(channels)[:, None] == source[None, :]).astype(BF)

    pre_one = conv(inputs, first_filter, s1)
    hidden = (inputs.astype(F32) + jax.nn.silu(pre_one)).astype(BF)
    pre_two = conv(hidden, second_filter, s2)
    second_delta = (upstream * silu_grad(pre_two)).astype(BF)
    hidden_grad = upstream + conv_back(second_delta, second_filter, s2)
    first_delta = (hidden_grad * silu_grad(pre_one)).astype(BF)
    input_grad = (hidden_grad + conv_back(first_delta, first_filter, s1)).astype(BF)
    input_grad = regroup(input_grad, n_seq)

    two = filter_share(hidden, second_delta, s2, mine, n_seq, n_hosp)
    one = filter_share(inputs, first_delta, s1, mine, n_seq, n_hosp)
    depth = channels // n_seq
    pieces = n_hosp // 2
    both = jnp.concatenate([one, two], axis=0).reshape(6, depth, pieces, width)
    both = both.transpose(2, 0, 1, 3)
    same_core = [[2 * p + c for p in range(pieces)] for c in range(2)]
    both = lax.all_to_all(both, "hosp", 0, 0, axis_index_groups=same_core)
    both = jnp.sum(both.astype(F32), axis=0)
    both = both * (1.0 / math.sqrt(n_hosp * rows * n_seq))
    both = both.transpose(1, 0, 2)
    return (input_grad[None], both[:, :3], both[:, 3:])


def solution(mesh):
    in_specs = (P("hosp", "seq", None), P("hosp", "seq", None), P(), P())
    out_specs = (P("hosp", "seq", None), P("seq", None, "hosp"), P("seq", None, "hosp"))
    return jax.shard_map(
        per_device, mesh=mesh, in_specs=in_specs, out_specs=out_specs, check_vma=False
    )
```

time: 692 us -> 158 us (0.23)
  waiting for transfers between devices: 595 us -> 71.5 us
  between operations: 15.5 us -> 1 us
    unnamed x4 -> x0, waiting for transfers between devices: 526 us -> none
    all_to_all x0 -> x6, waiting for transfers between devices: none -> 69.3 us  [the longest x3 29.5 us: regroup(): return lax.all_to_all(parts, 'seq', 0, 0).reshape(rows, channels)]
    ppermute x10 -> x2, waiting for transfers between devices: 68.9 us -> 2.25 us  [filter_share(): other = lax.ppermute(terms[:, :, half:].astype(BF), 'hosp', swap)]
    all_to_all x0 -> x6, starting transfers between devices: none -> 49.5 us  [the longest x3 23.3 us: regroup(): return lax.all_to_all(parts, 'seq', 0, 0).reshape(rows, channels)]
    ppermute x10 -> x2, starting transfers between devices: 46.6 us -> 3.97 us  [filter_share(): other = lax.ppermute(terms[:, :, half:].astype(BF), 'hosp', swap)]
    convert_element_type x4 -> x0, local copies, waits for them, and re-layouts: 8.72 us -> none  [the longest x2 6.08 us: reduce_filters(): jnp.einsum('tki,to->iko', stack, delta, preferred_element_type=jnp.float32)]
    dot_general x6 -> x20, matrix products: 18 us -> 17.3 us  [the longest x8 7.67 us: dot(): return jnp.dot(a, b, preferred_element_type=F32)]
  transfers between devices with their start and end apart: 12 -> 8, of which waited for: 10 -> 7; matrix products, arithmetic and copies ran while one was open for 2% -> 11% of each run, Pallas kernels for 0% -> 0%
where the time goes in v1:
time: 158 us; the launch traced here: 156 us
  waiting for transfers between devices  71.5 us (45%)
  starting transfers between devices  53.4 us (34%)
  matrix products  17.3 us (11%)
  local copies, waits for them, and re-layouts  9.52 us (6%)
  other arithmetic  2.72 us (2%)
    all_to_all x3, waiting for transfers between devices, regroup(): return lax.all_to_all(parts, 'seq', 0, 0).reshape(rows, channels)  29.5 us
    all_to_all x2, waiting for transfers between devices, filter_share(): pair = lax.all_to_all(pair, 'seq', 0, 0)  27.4 us
    all_to_all x3, starting transfers between devices, regroup(): return lax.all_to_all(parts, 'seq', 0, 0).reshape(rows, channels)  23.3 us
    all_to_all x2, starting transfers between devices, filter_share(): pair = lax.all_to_all(pair, 'seq', 0, 0)  13.2 us
    all_to_all x1, starting transfers between devices, per_device(): both = lax.all_to_all(both, 'hosp', 0, 0, axis_index_groups=same_core)  12.9 us
    all_to_all x1, waiting for transfers between devices, per_device(): both = lax.all_to_all(both, 'hosp', 0, 0, axis_index_groups=same_core)  12.5 us
    dot_general x8, matrix products, dot(): return jnp.dot(a, b, preferred_element_type=F32)  7.67 us
    unnamed x29, local copies, waits for them, and re-layouts  6.35 us
  transfers between devices with their start and end apart: 8, of which 7 were waited for; matrix products, arithmetic and copies ran while one was open for 11% of the time, Pallas kernels for 0%

profile of v1, /device:TPU:6, one launch (start us, length us, event | category | flops | bytes accessed | tf_op | source)
XLA Modules:
  0.0 155.6 jit_solution(18275727037813415247)
XLA Ops:
  0.6 10.4 %all-to-all-start.1 = ((bf16[16,32,512]{2,1,0:T(8,128)(2,1)}), bf16[16,32,512]{2,1,0:T(8,128)(2,1)S(1)}, u32[]{:S(2)}, u32[]{:S(2)}) async-start(bf16[16,32,512]{2,1,0:T(8,128)(2,1)} %bitcast.103), calls=%async_computation.1 | async-start | bytes 1048576 | tf_op jit(solution)/shard_map/all_to_all | solution.py:22
  11.0 13.5 %all-to-all-done.1 = bf16[16,32,512]{2,1,0:T(8,128)(2,1)S(1)} async-done(((bf16[16,32,512]{2,1,0:T(8,128)(2,1)}), bf16[16,32,512]{2,1,0:T(8,128)(2,1)S(1)}, u32[]{:S(2)}, u32[]{:S(2)}) %all-to-all-start.1) | async-done | bytes 524320 | tf_op jit(solution)/shard_map/all_to_all | solution.py:22
  24.5 6.4 %all-to-all-start = ((bf16[16,32,512]{2,1,0:T(8,128)(2,1)}), bf16[16,32,512]{2,1,0:T(8,128)(2,1)}, u32[]{:S(2)}, u32[]{:S(2)}) async-start(bf16[16,32,512]{2,1,0:T(8,128)(2,1)} %bitcast.104), calls=%async_computation | async-start | bytes 1048576 | tf_op jit(solution)/shard_map/all_to_all | solution.py:22
  32.6 1.6 %add_convert_fusion = (bf16[512,512]{1,0:T(8,128)(2,1)S(1)}, f32[512,512]{1,0:T(8,128)}) fusion(bf16[16,32,512]{2,1,0:T(8,128)(2,1)S(1)} %all-to-all-done.1, f32[512,512]{1,0:T(8,128)S(1)} %convolution_add_fusion.7, bf16[3,512,512]{2,1,0:T(8,128)(2,1)S(1)} %copy-done, bf16[448,512]{1,0:T(8,128)(2,1)S(1)} %bitcast.99), kind=kOutput, calls=%fused_computation.31 | convolution fusion | flops 270532608 | bytes 4128768 | tf_op jit(solution)/shard_map/dot_general | solution.py:34
  34.3 1.5 copy-done.7
  36.3 1.4 convolution_add_fusion.5
  37.7 6.1 %all-to-all-done = bf16[16,32,512]{2,1,0:T(8,128)(2,1)} async-done(((bf16[16,32,512]{2,1,0:T(8,128)(2,1)}), bf16[16,32,512]{2,1,0:T(8,128)(2,1)}, u32[]{:S(2)}, u32[]{:S(2)}) %all-to-all-start) | async-done | bytes 524320 | tf_op jit(solution)/shard_map/all_to_all | solution.py:22
  43.8 2.4 %fusion.5 = bf16[512,512]{1,0:T(8,128)(2,1)S(1)} fusion(bf16[512,512]{1,0:T(8,128)(2,1)} %bitcast.2, f32[512,512]{1,0:T(8,128)} %convolution_add_fusion.5, bf16[384,512]{1,0:T(8,128)(2,1)S(1)} %slice.103, bf16[3,512,512]{2,1,0:T(8,128)(2,1)} %param.7), kind=kOutput, calls=%fused_computation.28 | convolution fusion | flops 271319040 | bytes 3014656 | tf_op jit(solution)/shard_map/dot_general | solution.py:34
  49.4 2.1 %collective-permute-start.1 = (bf16[3,512,256]{2,1,0:T(8,128)(2,1)S(1)}, bf16[3,512,256]{2,1,0:T(8,128)(2,1)S(1)}, u32[]{:S(2)}, u32[]{:S(2)}) collective-permute-start(bf16[3,512,256]{2,1,0:T(8,128)(2,1)S(1)} %slice.170), channel_id=1, source_target_pairs={{0,16},{16,0},{32,48},{48,32},{64,80},{80,64},{96,112},{112,96},{1... | collective-permute-start | bytes 2359304 | tf_op jit(solution)/shard_map/ppermute | solution.py:66
  51.9 2.8 %multiply_convert_fusion = (bf16[512,512]{1,0:T(8,128)(2,1)S(1)}, f32[512,512]{1,0:T(8,128)}) fusion(f32[512,512]{1,0:T(8,128)S(1)} %copy-done.12, f32[512,512]{1,0:T(8,128)S(1)} %convolution_add_fusion.3, bf16[3,512,512]{2,1,0:T(8,128)(2,1)S(1)} %copy-done.8, bf16[384,512]{1,0:T(8,128)(2,1)S(1)} %slice-done.1, bf16[512,512]{1,0:T(8,128)(2,1)} %bitcast.2), kind=kOutput, calls=%fused_computation.30 | convolution fusion | flops 271581184 | bytes 5111808 | tf_op jit(solution)/shard_map/dot_general | solution.py:44
  55.9 1.4 convolution_bitcast_fusion.3
  58.6 6.4 %all-to-all-start.4 = ((bf16[16,3,32,256]{3,2,1,0:T(8,128)(2,1)}), bf16[16,3,32,256]{3,2,1,0:T(8,128)(2,1)}, u32[]{:S(2)}, u32[]{:S(2)}) async-start(bf16[16,3,32,256]{3,2,1,0:T(8,128)(2,1)} %bitcast.94), calls=%async_computation.4 | async-start | bytes 1572864 | tf_op jit(solution)/shard_map/all_to_all | solution.py:70
  66.6 1.9 %collective-permute-start = (bf16[3,512,256]{2,1,0:T(8,128)(2,1)S(1)}, bf16[3,512,256]{2,1,0:T(8,128)(2,1)S(1)}, u32[]{:S(2)}, u32[]{:S(2)}) collective-permute-start(bf16[3,512,256]{2,1,0:T(8,128)(2,1)S(1)} %slice.171), channel_id=1, source_target_pairs={{0,16},{16,0},{32,48},{48,32},{64,80},{80,64},{96,112},{112,96},{1... | collective-permute-start | bytes 2359304 | tf_op jit(solution)/shard_map/ppermute | solution.py:66
  68.5 2.3 %collective-permute-done = bf16[3,512,256]{2,1,0:T(8,128)(2,1)S(1)} collective-permute-done((bf16[3,512,256]{2,1,0:T(8,128)(2,1)S(1)}, bf16[3,512,256]{2,1,0:T(8,128)(2,1)S(1)}, u32[]{:S(2)}, u32[]{:S(2)}) %collective-permute-start) | collective-permute-done | bytes 786464 | tf_op jit(solution)/shard_map/ppermute | solution.py:66
  71.1 0.9 copy.19
  72.1 12.2 %all-to-all-done.4 = bf16[16,3,32,256]{3,2,1,0:T(8,128)(2,1)} async-done(((bf16[16,3,32,256]{3,2,1,0:T(8,128)(2,1)}), bf16[16,3,32,256]{3,2,1,0:T(8,128)(2,1)}, u32[]{:S(2)}, u32[]{:S(2)}) %all-to-all-start.4) | async-done | bytes 786464 | tf_op jit(solution)/shard_map/all_to_all | solution.py:70
  84.3 6.8 %all-to-all-start.3 = ((bf16[16,3,32,256]{3,2,1,0:T(8,128)(2,1)}), bf16[16,3,32,256]{3,2,1,0:T(8,128)(2,1)S(1)}, u32[]{:S(2)}, u32[]{:S(2)}) async-start(bf16[16,3,32,256]{3,2,1,0:T(8,128)(2,1)} %bitcast.95), calls=%async_computation.3 | async-start | bytes 1572864 | tf_op jit(solution)/shard_map/all_to_all | solution.py:70
  92.9 1.3 fusion.4
  94.1 15.2 %all-to-all-done.3 = bf16[16,3,32,256]{3,2,1,0:T(8,128)(2,1)S(1)} async-done(((bf16[16,3,32,256]{3,2,1,0:T(8,128)(2,1)}), bf16[16,3,32,256]{3,2,1,0:T(8,128)(2,1)S(1)}, u32[]{:S(2)}, u32[]{:S(2)}) %all-to-all-start.3) | async-done | bytes 786464 | tf_op jit(solution)/shard_map/all_to_all | solution.py:70
  109.3 6.6 %all-to-all-start.2 = ((bf16[16,32,512]{2,1,0:T(8,128)(2,1)}), bf16[16,32,512]{2,1,0:T(8,128)(2,1)S(1)}, u32[]{:S(2)}, u32[]{:S(2)}) async-start(bf16[16,32,512]{2,1,0:T(8,128)(2,1)} %bitcast.13), calls=%async_computation.2 | async-start | bytes 1048576 | tf_op jit(solution)/shard_map/all_to_all | solution.py:22
  115.9 1.3 reduce_sum.34
  118.5 9.9 %all-to-all-done.2 = bf16[16,32,512]{2,1,0:T(8,128)(2,1)S(1)} async-done(((bf16[16,32,512]{2,1,0:T(8,128)(2,1)}), bf16[16,32,512]{2,1,0:T(8,128)(2,1)S(1)}, u32[]{:S(2)}, u32[]{:S(2)}) %all-to-all-start.2) | async-done | bytes 524320 | tf_op jit(solution)/shard_map/all_to_all | solution.py:22
  128.4 12.9 %all-to-all-start.5 = ((bf16[16,2,1536]{2,1,0:T(2,128)(2,1)}), bf16[16,2,1536]{2,1,0:T(2,128)(2,1)S(1)}, u32[]{:S(2)}, u32[]{:S(2)}) async-start(bf16[16,2,1536]{2,1,0:T(2,128)(2,1)} %reshape.74), calls=%async_computation.5 | async-start | bytes 196608 | tf_op jit(solution)/shard_map/all_to_all | solution.py:107
  141.3 12.5 %all-to-all-done.5 = bf16[16,2,1536]{2,1,0:T(2,128)(2,1)S(1)} async-done(((bf16[16,2,1536]{2,1,0:T(2,128)(2,1)}), bf16[16,2,1536]{2,1,0:T(2,128)(2,1)S(1)}, u32[]{:S(2)}, u32[]{:S(2)}) %all-to-all-start.5) | async-done | bytes 98336 | tf_op jit(solution)/shard_map/all_to_all | solution.py:107
  (68 shorter events, 15.0 us)
Async XLA Ops:
  0.6 30.3 %copy-start = (bf16[3,512,512]{2,1,0:T(8,128)(2,1)S(1)}, bf16[3,512,512]{2,1,0:T(8,128)(2,1)}, u32[]{:S(2)}) copy-start(bf16[3,512,512]{2,1,0:T(8,128)(2,1)} %param.6) | copy-start | bytes 4718596
  0.6 23.9 %all-to-all-start.1 = ((bf16[16,32,512]{2,1,0:T(8,128)(2,1)}), bf16[16,32,512]{2,1,0:T(8,128)(2,1)S(1)}, u32[]{:S(2)}, u32[]{:S(2)}) async-start(bf16[16,32,512]{2,1,0:T(8,128)(2,1)} %bitcast.103), calls=%async_computation.1 | async-start | bytes 1048576 | tf_op jit(solution)/shard_map/all_to_all | solution.py:22
  24.5 19.2 %all-to-all-start = ((bf16[16,32,512]{2,1,0:T(8,128)(2,1)}), bf16[16,32,512]{2,1,0:T(8,128)(2,1)}, u32[]{:S(2)}, u32[]{:S(2)}) async-start(bf16[16,32,512]{2,1,0:T(8,128)(2,1)} %bitcast.104), calls=%async_computation | async-start | bytes 1048576 | tf_op jit(solution)/shard_map/all_to_all | solution.py:22
  31.9 0.8 copy-start.9
  34.3 1.6 %copy-start.7 = (bf16[3,512,512]{2,1,0:T(8,128)(2,1)S(1)}, bf16[3,512,512]{2,1,0:T(8,128)(2,1)}, u32[]{:S(2)}) copy-start(bf16[3,512,512]{2,1,0:T(8,128)(2,1)} %param.7) | copy-start | bytes 4718596
  34.3 2.0 %copy-start.4 = (bf16[448,512]{1,0:T(8,128)(2,1)}, bf16[448,512]{1,0:T(8,128)(2,1)S(1)}, u32[]{:S(2)}) copy-start(bf16[448,512]{1,0:T(8,128)(2,1)S(1)} %slice.102) | copy-start | bytes 1376260
  43.8 2.4 %copy-start.8 = (bf16[3,512,512]{2,1,0:T(8,128)(2,1)S(1)}, bf16[3,512,512]{2,1,0:T(8,128)(2,1)}, u32[]{:S(2)}) copy-start(bf16[3,512,512]{2,1,0:T(8,128)(2,1)} %param.7) | copy-start | bytes 4718596
  46.1 0.8 copy-start.6
  46.9 1.0 copy-start.5
  49.2 2.2 %slice-start = ((bf16[512,512]{1,0:T(8,128)(2,1)}), bf16[448,512]{1,0:T(8,128)(2,1)S(1)}, s32[]{:S(2)}) async-start(bf16[512,512]{1,0:T(8,128)(2,1)} %copy-done.6), calls=%async_computation.6 | async-start | bytes 917504 | tf_op jit(solution)/shard_map/slice | solution.py:30
  49.3 2.6 %slice-start.1 = ((bf16[512,512]{1,0:T(8,128)(2,1)}), bf16[384,512]{1,0:T(8,128)(2,1)S(1)}, s32[]{:S(2)}) async-start(bf16[512,512]{1,0:T(8,128)(2,1)} %copy-done.6), calls=%async_computation.7 | async-start | bytes 786432 | tf_op jit(solution)/shard_map/slice | solution.py:30
  49.4 2.6 %copy-start.12 = (f32[512,512]{1,0:T(8,128)S(1)}, f32[512,512]{1,0:T(8,128)}, u32[]{:S(2)}) copy-start(f32[512,512]{1,0:T(8,128)} %get-tuple-element.6) | copy-start | bytes 3145732
  49.4 8.0 %collective-permute-start.1 = (bf16[3,512,256]{2,1,0:T(8,128)(2,1)S(1)}, bf16[3,512,256]{2,1,0:T(8,128)(2,1)S(1)}, u32[]{:S(2)}, u32[]{:S(2)}) collective-permute-start(bf16[3,512,256]{2,1,0:T(8,128)(2,1)S(1)} %slice.170), channel_id=1, source_target_pairs={{0,16},{16,0},{32,48},{48,32},{64,80},{80,64},{96,112},{112,96},{1... | collective-permute-start | bytes 2359304 | tf_op jit(solution)/shard_map/ppermute | solution.py:66
  54.7 2.6 %copy-start.2 = (bf16[512,512]{1,0:T(8,128)(2,1)}, bf16[512,512]{1,0:T(8,128)(2,1)S(1)}, u32[]{:S(2)}) copy-start(bf16[512,512]{1,0:T(8,128)(2,1)S(1)} %get-tuple-element.7) | copy-start | bytes 1572868
  54.7 1.2 copy-start.10
  58.6 25.7 %all-to-all-start.4 = ((bf16[16,3,32,256]{3,2,1,0:T(8,128)(2,1)}), bf16[16,3,32,256]{3,2,1,0:T(8,128)(2,1)}, u32[]{:S(2)}, u32[]{:S(2)}) async-start(bf16[16,3,32,256]{3,2,1,0:T(8,128)(2,1)} %bitcast.94), calls=%async_computation.4 | async-start | bytes 1572864 | tf_op jit(solution)/shard_map/all_to_all | solution.py:70
  65.0 1.2 copy-start.1
  66.6 4.2 %collective-permute-start = (bf16[3,512,256]{2,1,0:T(8,128)(2,1)S(1)}, bf16[3,512,256]{2,1,0:T(8,128)(2,1)S(1)}, u32[]{:S(2)}, u32[]{:S(2)}) collective-permute-start(bf16[3,512,256]{2,1,0:T(8,128)(2,1)S(1)} %slice.171), channel_id=1, source_target_pairs={{0,16},{16,0},{32,48},{48,32},{64,80},{80,64},{96,112},{112,96},{1... | collective-permute-start | bytes 2359304 | tf_op jit(solution)/shard_map/ppermute | solution.py:66
  71.1 20.0 %copy-start.3 = (bf16[512,512]{1,0:T(8,128)(2,1)S(1)}, bf16[512,512]{1,0:T(8,128)(2,1)}, u32[]{:S(2)}) copy-start(bf16[512,512]{1,0:T(8,128)(2,1)} %copy-done.2) | copy-start | bytes 1572868
  84.3 25.0 %all-to-all-start.3 = ((bf16[16,3,32,256]{3,2,1,0:T(8,128)(2,1)}), bf16[16,3,32,256]{3,2,1,0:T(8,128)(2,1)S(1)}, u32[]{:S(2)}, u32[]{:S(2)}) async-start(bf16[16,3,32,256]{3,2,1,0:T(8,128)(2,1)} %bitcast.95), calls=%async_computation.3 | async-start | bytes 1572864 | tf_op jit(solution)/shard_map/all_to_all | solution.py:70
  91.7 1.2 copy-start.11
  109.3 19.1 %all-to-all-start.2 = ((bf16[16,32,512]{2,1,0:T(8,128)(2,1)}), bf16[16,32,512]{2,1,0:T(8,128)(2,1)S(1)}, u32[]{:S(2)}, u32[]{:S(2)}) async-start(bf16[16,32,512]{2,1,0:T(8,128)(2,1)} %bitcast.13), calls=%async_computation.2 | async-start | bytes 1048576 | tf_op jit(solution)/shard_map/all_to_all | solution.py:22
  128.4 25.4 %all-to-all-start.5 = ((bf16[16,2,1536]{2,1,0:T(2,128)(2,1)}), bf16[16,2,1536]{2,1,0:T(2,128)(2,1)S(1)}, u32[]{:S(2)}, u32[]{:S(2)}) async-start(bf16[16,2,1536]{2,1,0:T(2,128)(2,1)} %reshape.74), calls=%async_computation.5 | async-start | bytes 196608 | tf_op jit(solution)/shard_map/all_to_all | solution.py:107

commit v2 on v0

v2 whole, which is shorter than its diff:
```python
import math

import jax
import jax.numpy as jnp
from jax import lax
from jax.experimental import pallas as pl
from jax.experimental.pallas import tpu as pltpu
from jax.sharding import PartitionSpec as P

FIRST_DILATION = 512
SECOND_DILATION = 1024
BF = jnp.bfloat16
F32 = jnp.float32
ZH, NY, NC, ZL, NX = 2, 8, 2, 4, 4
NS = ZL * NX
NZ = ZH * ZL
C = 512
R = 512
SUB = R // NS
S1 = FIRST_DILATION // NS
S2 = SECOND_DILATION // NS
HALF = C // NC
YW = HALF // NY
ZW = YW // ZH
XW = C // NX
STEP = 256


def silu_grad(value):
    sigma = jax.nn.sigmoid(value)
    return sigma * (1.0 + value * (1.0 - sigma))


def nn(a, b):
    return jnp.dot(a, b, preferred_element_type=F32)


def nt(a, b):
    return lax.dot_general(a, b, (((1,), (1,)), ((), ())), preferred_element_type=F32)


def over_rows(body):
    def step(c, carry):
        body(pl.multiple_of(c * STEP, STEP))
        return carry

    lax.fori_loop(0, R // STEP, step, 0)


def kernel(
    frames, cot, w1, w2, perm_i, perm_o,
    out, grads,
    fp, hp, fq, hq, d1, d2, cots, g1, g2, hg, ig, tt,
    mine, other, got, s0, ry2, sx2, rx2, rx1, sy1, ry1, s2, rz,
    sem_f, sem_c, sem_g, sem_w, sem_y2, sem_x2, sem_x1, sem_y1, sem_z,
):
    h = lax.axis_index("hosp")
    s = lax.axis_index("seq")
    core = lax.rem(h, NC)
    y = lax.rem(lax.div(h, NC), NY)
    zh = lax.div(h, NC * NY)
    x = lax.rem(s, NX)
    zl = lax.div(s, NX)
    z = zh * ZL + zl

    def seq_dev(t):
        return (h, t)

    def x_dev(t):
        return (h, zl * NX + t)

    def y_dev(t):
        return ((zh * NY + t) * NC + core, s)

    def z_dev(t):
        return ((lax.div(t, ZL) * NY + y) * NC + core, lax.rem(t, ZL) * NX + x)

    partner = (h + 1 - 2 * core, s)
    barrier = pltpu.get_barrier_semaphore()

    def greet(dev):
        pl.semaphore_signal(barrier, inc=1, device_id=dev, device_id_type=pl.DeviceIdType.MESH)

    def loop(first, last, body):
        def step(r, carry):
            body(r)
            return carry

        lax.fori_loop(first, last, step, 0)

    loop(1, NS, lambda r: greet(seq_dev(lax.rem(s + r, NS))))
    loop(1, NY, lambda r: greet(y_dev(lax.rem(y + r, NY))))
    loop(0, ZL, lambda r: greet(z_dev((1 - zh) * ZL + r)))
    greet(partner)
    pl.semaphore_wait(barrier, NS - 1 + NY - 1 + ZL + 1)

    class Exchange:
        def __init__(self, n, me, dev, src, dst, sem):
            self.n, self.me, self.dev, self.src, self.dst, self.sem = n, me, dev, src, dst, sem

        def copy(self, r, to, slot):
            return pltpu.make_async_remote_copy(
                src_ref=self.src(to), dst_ref=self.dst(slot),
                send_sem=self.sem.at[0, r], recv_sem=self.sem.at[1, r],
                device_id=self.dev(to), device_id_type=pl.DeviceIdType.MESH,
            )

        def push(self):
            loop(1, self.n, lambda r: self.copy(r, lax.rem(self.me + r, self.n), self.me).start())

        def land(self):
            def body(r):
                slot = lax.rem(self.me + self.n - r, self.n)
                self.copy(r, lax.rem(self.me + r, self.n), slot).wait_recv()

            loop(1, self.n, body)

        def sent(self):
            loop(1, self.n, lambda r: self.copy(r, lax.rem(self.me + r, self.n), self.me).wait_send())

    def rows_at(base):
        return lambda t: pl.ds(pl.multiple_of(base + t * SUB, SUB), SUB)

    at_f = rows_at(2 * S1)
    at_0 = rows_at(0)
    ex_f = Exchange(NS, s, seq_dev, lambda t: frames.at[at_0(t)], lambda t: fp.at[at_f(t)], sem_f)
    ex_c = Exchange(NS, s, seq_dev, lambda t: cot.at[at_0(t)], lambda t: cots.at[at_0(t)], sem_c)
    ex_g = Exchange(NS, s, seq_dev, lambda t: ig.at[at_0(t)], lambda t: out.at[at_0(t)], sem_g)

    def at_y(t):
        return pl.ds(pl.multiple_of(t * YW, YW), YW)

    def at_x(t):
        return pl.ds(pl.multiple_of(t * XW, XW), XW)

    def at_z(t):
        return pl.ds(pl.multiple_of(lax.div(t, ZL) * ZW, ZW), ZW)

    ex_y2 = Exchange(NY, y, y_dev, lambda t: s0.at[1, :, at_y(t), :], lambda t: ry2.at[t], sem_y2)
    ex_x2 = Exchange(NX, x, x_dev, lambda t: sx2.at[:, :, at_x(t)], lambda t: rx2.at[t], sem_x2)
    ex_x1 = Exchange(NX, x, x_dev, lambda t: s0.at[0, :, :, at_x(t)], lambda t: rx1.at[t], sem_x1)
    ex_y1 = Exchange(NY, y, y_dev, lambda t: sy1.at[:, at_y(t), :], lambda t: ry1.at[t], sem_y1)
    ex_z = Exchange(NZ, z, z_dev, lambda t: s2.at[:, at_z(t), :], lambda t: rz.at[t], sem_z)

    ex_f.push()
    ex_c.push()

    fp[0 : 2 * S1, :] = jnp.zeros((2 * S1, C), BF)
    fq[0 : 2 * S1, :] = jnp.zeros((2 * S1, C), BF)
    hp[0 : 2 * S2, :] = jnp.zeros((2 * S2, C), BF)
    hq[0 : 2 * S2, :] = jnp.zeros((2 * S2, C), BF)
    d1[R : R + 2 * S1, :] = jnp.zeros((2 * S1, C), BF)
    d2[R : R + 2 * S2, :] = jnp.zeros((2 * S2, C), BF)
    fp[at_f(s), :] = frames[at_0(s), :]
    cots[at_0(s), :] = cot[at_0(s), :]

    def rows(ref, start, size=STEP):
        return ref[pl.ds(pl.multiple_of(start, SUB), size), :]

    def put(ref, start, value):
        ref[pl.ds(pl.multiple_of(start, SUB), STEP), :] = value

    ex_f.land()

    def forward_one(c):
        base = 2 * S1 + c
        here = rows(fp, base)
        pre = nn(here, w1[0]) + nn(rows(fp, base - S1), w1[1]) + nn(rows(fp, base - 2 * S1), w1[2])
        sigma = jax.nn.sigmoid(pre)
        put(g1, c, sigma * (1.0 + pre * (1.0 - sigma)))
        put(hp, 2 * S2 + c, (here.astype(F32) + pre * sigma).astype(BF))

    over_rows(forward_one)

    def forward_two(c):
        base = 2 * S2 + c
        pre = (
            nn(rows(hp, base), w2[0]) + nn(rows(hp, base - S2), w2[1])
            + nn(rows(hp, base - 2 * S2), w2[2])
        )
        put(g2, c, silu_grad(pre))

    over_rows(forward_two)

    def reorder(c):
        put(fq, 2 * S1 + c, nn(rows(fp, 2 * S1 + c), perm_i[...]).astype(BF))
        put(hq, 2 * S2 + c, nn(rows(hp, 2 * S2 + c), perm_i[...]).astype(BF))

    over_rows(reorder)

    ex_c.land()

    def second_delta(c):
        put(d2, c, (rows(cots, c).astype(F32) * rows(g2, c)).astype(BF))

    over_rows(second_delta)

    def swap(layer, k):
        return pltpu.make_async_remote_copy(
            src_ref=other.at[layer, k], dst_ref=got.at[layer, k],
            send_sem=sem_w.at[0, layer, k], recv_sem=sem_w.at[1, layer, k],
            device_id=partner, device_id_type=pl.DeviceIdType.MESH,
        )

    def terms(layer, delta, source, pad, shift):
        def turn(c):
            put(tt, c, nt(rows(perm_o, c), delta[0:R, :]).astype(BF))

        over_rows(turn)

        def theirs(k):
            taps = rows(source, pad - k * shift, R)
            other[layer, k] = nn(tt[HALF:, :], taps).astype(BF)
            swap(layer, k).start()

        loop(0, 3, theirs)

        def ours(k):
            mine[k] = nn(tt[:HALF, :], rows(source, pad - k * shift, R))

        loop(0, 3, ours)

    def pair_sum(layer):
        def one(k):
            swap(layer, k).wait_recv()
            s0[layer, k] = (mine[k] + got[layer, k].astype(F32)).astype(BF)

        loop(0, 3, one)

    terms(1, d2, hq, 2 * S2, S2)
    pair_sum(1)
    ex_y2.push()

    def first_delta(c):
        value = (
            rows(cots, c).astype(F32) + nt(rows(d2, c), w2[0]) + nt(rows(d2, c + S2), w2[1])
            + nt(rows(d2, c + 2 * S2), w2[2])
        )
        put(hg, c, value)
        put(d1, c, (value * rows(g1, c)).astype(BF))

    over_rows(first_delta)
    terms(0, d1, fq, 2 * S1, S1)

    def input_grad(c):
        value = (
            rows(hg, c) + nt(rows(d1, c), w1[0]) + nt(rows(d1, c + S1), w1[1])
            + nt(rows(d1, c + 2 * S1), w1[2])
        )
        put(ig, c, value.astype(BF))

    pair_sum(0)
    ex_x1.push()
    over_rows(input_grad)
    ex_g.push()
    out[at_0(s), :] = ig[at_0(s), :]

    def gather(ex, own, n, me):
        ex.dst(me)[...] = own
        ex.land()
        ref = ex.dst
        total = ref(0)[...].astype(F32)
        for t in range(1, n):
            total = total + ref(t)[...].astype(F32)
        return total

    sx2[...] = gather(ex_y2, s0[1, :, at_y(y), :], NY, y).astype(BF)
    ex_x2.push()
    sy1[...] = gather(ex_x1, s0[0, :, :, at_x(x)], NX, x).astype(BF)
    ex_y1.push()
    s2[3:6] = gather(ex_x2, sx2[:, :, at_x(x)], NX, x).astype(BF)
    s2[0:3] = gather(ex_y1, sy1[:, at_y(y), :], NY, y).astype(BF)
    ex_z.push()
    grads[...] = gather(ex_z, s2[:, at_z(z), :], NZ, z)
    ex_g.land()

    for ex in (ex_f, ex_c, ex_g, ex_y2, ex_x2, ex_x1, ex_y1, ex_z):
        ex.sent()
    loop(0, 3, lambda k: swap(0, k).wait_send())
    loop(0, 3, lambda k: swap(1, k).wait_send())


def per_device(frames, cotangent, first_filter, second_filter):
    core = lax.axis_index("hosp") % NC
    zl = lax.axis_index("seq") // NX
    a = jnp.arange(C)
    width = C // NS
    i_from = ((a // width) % ZL) * (NX * width) + (a // (ZL * width)) * width + a % width
    perm_i = (a[:, None] == i_from[None, :]).astype(BF)
    owner = jnp.where(a < HALF, core, 1 - core)
    b = a % HALF
    o_from = ((b // ZW) % ZH) * (NY * NC * ZW) + (b // YW) * (NC * ZW) + owner * ZW + b % ZW
    perm_o = (o_from[:, None] == a[None, :]).astype(BF)

    vmem = pl.BlockSpec(memory_space=pltpu.VMEM)
    dma = pltpu.SemaphoreType.DMA
    out, grads = pl.pallas_call(
        kernel,
        out_shape=(
            jax.ShapeDtypeStruct((R, C), BF),
            jax.ShapeDtypeStruct((6, ZW, XW), F32),
        ),
        in_specs=[vmem] * 6,
        out_specs=(vmem, vmem),
        scratch_shapes=[
            pltpu.VMEM((R + 2 * S1, C), BF),
            pltpu.VMEM((R + 2 * S2, C), BF),
            pltpu.VMEM((R + 2 * S1, C), BF),
            pltpu.VMEM((R + 2 * S2, C), BF),
            pltpu.VMEM((R + 2 * S1, C), BF),
            pltpu.VMEM((R + 2 * S2, C), BF),
            pltpu.VMEM((R, C), BF),
            pltpu.VMEM((R, C), F32),
            pltpu.VMEM((R, C), F32),
            pltpu.VMEM((R, C), F32),
            pltpu.VMEM((R, C), BF),
            pltpu.VMEM((C, R), BF),
            pltpu.VMEM((3, HALF, C), F32),
            pltpu.VMEM((2, 3, HALF, C), BF),
            pltpu.VMEM((2, 3, HALF, C), BF),
            pltpu.VMEM((2, 3, HALF, C), BF),
            pltpu.VMEM((NY, 3, YW, C), BF),
            pltpu.VMEM((3, YW, C), BF),
            pltpu.VMEM((NX, 3, YW, XW), BF),
            pltpu.VMEM((NX, 3, HALF, XW), BF),
            pltpu.VMEM((3, HALF, XW), BF),
            pltpu.VMEM((NY, 3, YW, XW), BF),
            pltpu.VMEM((6, YW, XW), BF),
            pltpu.VMEM((NZ, 6, ZW, XW), BF),
            dma((2, NS)),
            dma((2, NS)),
            dma((2, NS)),
            dma((2, 2, 3)),
            dma((2, NY)),
            dma((2, NX)),
            dma((2, NX)),
            dma((2, NY)),
            dma((2, NZ)),
        ],
        compiler_params=pltpu.CompilerParams(
            collective_id=0, has_side_effects=True, vmem_limit_bytes=48 * 1024 * 1024
        ),
    )(frames[0], cotangent[0], first_filter, second_filter, perm_i, perm_o)
    scale = 1.0 / math.sqrt(lax.axis_size("hosp") * R * lax.axis_size("seq"))
    own = lax.dynamic_slice_in_dim(grads, zl * width, width, axis=2) * scale
    own = own.transpose(2, 0, 1)
    return (out[None], own[:, :3], own[:, 3:])


def solution(mesh):
    in_specs = (P("hosp", "seq", None), P("hosp", "seq", None), P(), P())
    out_specs = (P("hosp", "seq", None), P("seq", None, "hosp"), P("seq", None, "hosp"))
    return jax.shard_map(
        per_device, mesh=mesh, in_specs=in_specs, out_specs=out_specs, check_vma=False
    )
```

time: 692 us -> 87.1 us (0.13)
  waiting for transfers between devices: 595 us -> 0 us
  Pallas kernels: 0 us -> 79.4 us
  starting transfers between devices: 46.6 us -> 0 us
  matrix products: 18 us -> 0 us
  between operations: 15.5 us -> 0.69 us
  local copies, waits for them, and re-layouts: 13.6 us -> 6.31 us
    unnamed x4 -> x0, waiting for transfers between devices: 526 us -> none
    pallas_call x0 -> x1, Pallas kernels: none -> 79.4 us  [per_device(): pl.pallas_call(kernel, out_shape=(jax.ShapeDtypeStruct((R, C), BF), jax.S...]
    ppermute x10 -> x0, waiting for transfers between devices: 68.9 us -> none  [passed_along(): return lax.ppermute(block, axis, route)]
    ppermute x10 -> x0, starting transfers between devices: 46.6 us -> none  [passed_along(): return lax.ppermute(block, axis, route)]
    dot_general x6 -> x0, matrix products: 18 us -> none  [the longest x2 7.85 us: back_grad(): jnp.einsum('tko,kio->ti', stack, filters, preferred_element_type=jnp.floa...]
    convert_element_type x4 -> x0, local copies, waits for them, and re-layouts: 8.72 us -> none  [the longest x2 6.08 us: reduce_filters(): jnp.einsum('tki,to->iko', stack, delta, preferred_element_type=jnp.float32)]
  transfers between devices with their start and end apart: 12 -> 0, of which waited for: 10 -> 0; matrix products, arithmetic and copies ran while one was open for 2% -> 0% of each run, Pallas kernels for 0% -> 0%
where the time goes in v2:
time: 87.1 us; the launch traced here: 86.8 us
  Pallas kernels  79.4 us (91%)
  local copies, waits for them, and re-layouts  6.31 us (7%)
    pallas_call x1, Pallas kernels, per_device(): pl.pallas_call(kernel, out_shape=(jax.ShapeDtypeStruct((R, C), BF), jax.S...  79.4 us
    unnamed x9, local copies, waits for them, and re-layouts  5.69 us

profile of v2, /device:TPU:6, one launch (start us, length us, event | category | flops | bytes accessed | tf_op | source)
XLA Modules:
  0.0 86.8 jit_solution(8359799833489967153)
XLA Ops:
  0.7 0.3 fusion
  1.0 0.0 copy-start
  1.0 1.4 %copy-done = bf16[3,512,512]{2,1,0:T(8,128)(2,1)S(1)} copy-done((bf16[3,512,512]{2,1,0:T(8,128)(2,1)S(1)}, bf16[3,512,512]{2,1,0:T(8,128)(2,1)}, u32[]{:S(2)}) %copy-start) | copy-done | bytes 1572888
  2.4 0.0 copy-start.1
  2.4 1.4 %copy-done.1 = bf16[3,512,512]{2,1,0:T(8,128)(2,1)S(1)} copy-done((bf16[3,512,512]{2,1,0:T(8,128)(2,1)S(1)}, bf16[3,512,512]{2,1,0:T(8,128)(2,1)}, u32[]{:S(2)}) %copy-start.1) | copy-done | bytes 1572888
  3.8 0.0 copy-start.2
  3.8 1.0 %copy-done.2 = bf16[1,512,512]{2,1,0:T(8,128)(2,1)S(1)} copy-done((bf16[1,512,512]{2,1,0:T(8,128)(2,1)S(1)}, bf16[1,512,512]{2,1,0:T(8,128)(2,1)}, u32[]{:S(2)}) %copy-start.2) | copy-done | bytes 524312
  4.8 0.0 copy-start.3
  4.8 1.0 %copy-done.3 = bf16[1,512,512]{2,1,0:T(8,128)(2,1)S(1)} copy-done((bf16[1,512,512]{2,1,0:T(8,128)(2,1)S(1)}, bf16[1,512,512]{2,1,0:T(8,128)(2,1)}, u32[]{:S(2)}) %copy-start.3) | copy-done | bytes 524312
  5.9 79.4 %shard_map.67 = (bf16[512,512]{1,0:T(8,128)(2,1)S(1)}, f32[6,16,128]{2,1,0:T(8,128)S(1)}) custom-call(bf16[512,512]{1,0:T(8,128)(2,1)S(1)} %bitcast.5, bf16[512,512]{1,0:T(8,128)(2,1)S(1)} %bitcast.6, bf16[3,512,512]{2,1,0:T(8,128)(2,1)S(1)} %copy-done, bf16[3,512,512]{2,1,0:T(8,128)(2,1)S(1)} %copy-done.1, bf16[512,512]{1,0:T(8,128)(2,1)S(1)} %get-tuple-element.9.perm_i, ...), custom_call_target="tpu_custom_call" | custom-call | tf_op jit(solution)/shard_map/pallas_call | solution.py:297
  85.3 0.1 multiply_bitcast_fusion
  85.4 0.6 fusion.27
  86.0 0.8 copy.8
  (2 shorter events, 0.0 us)
Async XLA Ops:
  1.0 1.4 %copy-start = (bf16[3,512,512]{2,1,0:T(8,128)(2,1)S(1)}, bf16[3,512,512]{2,1,0:T(8,128)(2,1)}, u32[]{:S(2)}) copy-start(bf16[3,512,512]{2,1,0:T(8,128)(2,1)} %w1.1) | copy-start | bytes 4718596
  2.4 1.4 %copy-start.1 = (bf16[3,512,512]{2,1,0:T(8,128)(2,1)S(1)}, bf16[3,512,512]{2,1,0:T(8,128)(2,1)}, u32[]{:S(2)}) copy-start(bf16[3,512,512]{2,1,0:T(8,128)(2,1)} %w2.1) | copy-start | bytes 4718596
  3.8 1.0 %copy-start.2 = (bf16[1,512,512]{2,1,0:T(8,128)(2,1)S(1)}, bf16[1,512,512]{2,1,0:T(8,128)(2,1)}, u32[]{:S(2)}) copy-start(bf16[1,512,512]{2,1,0:T(8,128)(2,1)} %param.4) | copy-start | bytes 1572868
  4.8 1.0 %copy-start.3 = (bf16[1,512,512]{2,1,0:T(8,128)(2,1)S(1)}, bf16[1,512,512]{2,1,0:T(8,128)(2,1)}, u32[]{:S(2)}) copy-start(bf16[1,512,512]{2,1,0:T(8,128)(2,1)} %param.5) | copy-start | bytes 1572868

commit v3 on v2

v3 whole, which is shorter than its diff:
```python
import math

import jax
import jax.numpy as jnp
from jax import lax
from jax.experimental import pallas as pl
from jax.experimental.pallas import tpu as pltpu
from jax.sharding import PartitionSpec as P

FIRST_DILATION = 512
SECOND_DILATION = 1024
BF = jnp.bfloat16
F32 = jnp.float32
ZH, NY, NC, ZL, NX = 2, 8, 2, 4, 4
NS = ZL * NX
NZ = ZH * ZL
C = 512
R = 512
PARTS = 1
M = R // PARTS
SUB = M // NS
S1 = FIRST_DILATION // NS // PARTS
S2 = SECOND_DILATION // NS // PARTS
HALF = C // NC
YW = HALF // NY
ZW = YW // ZH
XW = C // NX


def silu_grad(value):
    sigma = jax.nn.sigmoid(value)
    return sigma * (1.0 + value * (1.0 - sigma))


def nn(a, b):
    return jnp.dot(a, b, preferred_element_type=F32)


def nt(a, b):
    return lax.dot_general(a, b, (((1,), (1,)), ((), ())), preferred_element_type=F32)


def kernel(
    frames, cot, first, second, perm_i, perm_o,
    out, grads,
    fp, hp, fq, hq, d1, d2, cots, g1, g2, hg, ig, tt,
    acc, other, got, s0, sx, rx, sy, ry, s2, rz,
    w1, w2, w1t, w2t, sem_l,
    sem_f, sem_c, sem_g, sem_w, sem_x, sem_y, sem_z,
):
    h = lax.axis_index("hosp")
    s = lax.axis_index("seq")
    core = lax.rem(h, NC)
    y = lax.rem(lax.div(h, NC), NY)
    zh = lax.div(h, NC * NY)
    x = lax.rem(s, NX)
    zl = lax.div(s, NX)
    z = zh * ZL + zl

    def seq_dev(t):
        return (h, t)

    def x_dev(t):
        return (h, zl * NX + t)

    def y_dev(t):
        return ((zh * NY + t) * NC + core, s)

    def z_dev(t):
        return ((lax.div(t, ZL) * NY + y) * NC + core, lax.rem(t, ZL) * NX + x)

    partner = (h + 1 - 2 * core, s)
    loads = [
        pltpu.make_async_copy(src, dst, sem_l.at[i])
        for i, (src, dst) in enumerate(
            ((first, w1), (second, w2))
        )
    ]

    def at_part(t):
        return pl.ds(pl.multiple_of(t * SUB, SUB), SUB)

    def at_pad(t):
        return pl.ds(pl.multiple_of(2 * S1 + t * SUB, SUB), SUB)

    def at_full(p):
        return lambda t: pl.ds(pl.multiple_of(t * (PARTS * SUB) + p * SUB, SUB), SUB)

    own_f = [
        pltpu.make_async_copy(
            frames.at[at_full(p)(s)], fp.at[p, at_pad(s)], sem_l.at[4 + p]
        )
        for p in range(PARTS)
    ]
    own_c = [
        pltpu.make_async_copy(
            cot.at[at_full(p)(s)], cots.at[p, at_part(s)], sem_l.at[6 + p]
        )
        for p in range(PARTS)
    ]
    barrier = pltpu.get_barrier_semaphore()

    def greet(dev):
        pl.semaphore_signal(barrier, inc=1, device_id=dev, device_id_type=pl.DeviceIdType.MESH)

    def loop(first, last, body):
        def step(r, carry):
            body(r)
            return carry

        lax.fori_loop(first, last, step, 0)

    loop(1, NS, lambda r: greet(seq_dev(lax.rem(s + r, NS))))
    loop(1, NY, lambda r: greet(y_dev(lax.rem(y + r, NY))))
    loop(0, ZL, lambda r: greet(z_dev((1 - zh) * ZL + r)))
    greet(partner)
    pl.semaphore_wait(barrier, NS - 1 + NY - 1 + ZL + 1)

    class Exchange:
        def __init__(self, n, me, dev, src, dst, sem):
            self.n, self.me, self.dev, self.src, self.dst, self.sem = n, me, dev, src, dst, sem

        def copy(self, r, to, slot):
            return pltpu.make_async_remote_copy(
                src_ref=self.src(to), dst_ref=self.dst(slot),
                send_sem=self.sem.at[0, r], recv_sem=self.sem.at[1, r],
                device_id=self.dev(to), device_id_type=pl.DeviceIdType.MESH,
            )

        def push(self):
            loop(1, self.n, lambda r: self.copy(r, lax.rem(self.me + r, self.n), self.me).start())

        def land(self):
            def body(r):
                slot = lax.rem(self.me + self.n - r, self.n)
                self.copy(r, lax.rem(self.me + r, self.n), slot).wait_recv()

            loop(1, self.n, body)

        def sent(self):
            loop(1, self.n, lambda r: self.copy(r, lax.rem(self.me + r, self.n), self.me).wait_send())

    ex_f = [
        Exchange(NS, s, seq_dev, lambda t, p=p: frames.at[at_full(p)(t)],
                 lambda t, p=p: fp.at[p, at_pad(t)], sem_f.at[p])
        for p in range(PARTS)
    ]
    ex_c = [
        Exchange(NS, s, seq_dev, lambda t, p=p: cot.at[at_full(p)(t)],
                 lambda t, p=p: cots.at[p, at_part(t)], sem_c.at[p])
        for p in range(PARTS)
    ]
    ex_g = [
        Exchange(NS, s, seq_dev, lambda t, p=p: ig.at[p, at_part(t)],
                 lambda t, p=p: out.at[at_full(p)(t)], sem_g.at[p])
        for p in range(PARTS)
    ]

    def at_y(t):
        return pl.ds(pl.multiple_of(t * YW, YW), YW)

    def at_x(t):
        return pl.ds(pl.multiple_of(t * XW, XW), XW)

    def at_z(t):
        return pl.ds(pl.multiple_of(lax.div(t, ZL) * ZW, ZW), ZW)

    def y_stage(layer):
        return Exchange(
            NY, y, y_dev, lambda t: sy.at[layer, :, at_y(t), :], lambda t: ry.at[layer, t],
            sem_y.at[layer],
        )

    ex_y = (y_stage(0), y_stage(1))
    ex_z = Exchange(NZ, z, z_dev, lambda t: s2.at[:, at_z(t), :], lambda t: rz.at[t], sem_z)

    for p in range(PARTS):
        ex_f[p].push()
        ex_c[p].push()
        if p == 0:
            for load in (*loads, *own_f, *own_c):
                load.start()

    for p in range(PARTS):
        fp[p, 0 : 2 * S1, :] = jnp.zeros((2 * S1, C), BF)
        fq[p, 0 : 2 * S1, :] = jnp.zeros((2 * S1, C), BF)
        hp[p, 0 : 2 * S2, :] = jnp.zeros((2 * S2, C), BF)
        hq[p, 0 : 2 * S2, :] = jnp.zeros((2 * S2, C), BF)
        d1[p, M : M + 2 * S1, :] = jnp.zeros((2 * S1, C), BF)
        d2[p, M : M + 2 * S2, :] = jnp.zeros((2 * S2, C), BF)

    def behind(ref, p, shift):
        return jnp.concatenate([ref[p, j * shift : j * shift + M, :] for j in (2, 1, 0)], axis=1)

    def beyond(ref, p, shift):
        return jnp.concatenate([ref[p, j * shift : j * shift + M, :] for j in (0, 1, 2)], axis=1)

    def forward(p):
        own_f[p].wait()
        ex_f[p].land()
        here = fp[p, 2 * S1 :, :]
        pre = nn(behind(fp, p, S1), w1[...])
        sigma = jax.nn.sigmoid(pre)
        g1[p] = sigma * (1.0 + pre * (1.0 - sigma))
        hp[p, 2 * S2 :, :] = (here.astype(F32) + pre * sigma).astype(BF)
        g2[p] = silu_grad(nn(behind(hp, p, S2), w2[...]))
        fq[p, 2 * S1 :, :] = nn(here, perm_i[...]).astype(BF)
        hq[p, 2 * S2 :, :] = nn(hp[p, 2 * S2 :, :], perm_i[...]).astype(BF)

    def second_delta(p):
        own_c[p].wait()
        ex_c[p].land()
        d2[p, 0:M, :] = (cots[p].astype(F32) * g2[p]).astype(BF)

    def first_delta(p):
        value = cots[p].astype(F32) + nn(beyond(d2, p, S2), w2t[...])
        hg[p] = value
        d1[p, 0:M, :] = (value * g1[p]).astype(BF)

    def input_grad(p):
        ig[p] = (hg[p] + nn(beyond(d1, p, S1), w1t[...])).astype(BF)

    def send_grad(p):
        ex_g[p].push()
        out[at_full(p)(s), :] = ig[p, at_part(s), :]

    def swap(layer, k):
        return pltpu.make_async_remote_copy(
            src_ref=other.at[layer, k], dst_ref=got.at[layer, k],
            send_sem=sem_w.at[0, layer, k], recv_sem=sem_w.at[1, layer, k],
            device_id=partner, device_id_type=pl.DeviceIdType.MESH,
        )

    def taps(source, p, k, shift):
        return source[p, pl.ds(pl.multiple_of((2 - k) * shift, SUB), M), :]

    def turn(delta, p):
        tt[...] = nt(perm_o[...], delta[p, 0:M, :]).astype(BF)

    def terms(layer, delta, source, shift, between):
        turn(delta, 0)

        def theirs(k):
            value = nn(tt[HALF:, :], taps(source, 0, k, shift))
            other[layer, k] = value.astype(BF)
            swap(layer, k).start()

        loop(0, 3, theirs)
        between()

        def ours(k):
            acc[layer, k] = nn(tt[:HALF, :], taps(source, 0, k, shift))

        loop(0, 3, ours)

    def pair_sum(layer):
        def one(k):
            swap(layer, k).wait_recv()
            s0[layer, k] = (acc[layer, k] + got[layer, k].astype(F32)).astype(BF)

        loop(0, 3, one)

    right, left, far = (lax.rem(x + d, NX) for d in (1, NX - 1, NX // 2))
    low, high = pl.ds(0, HALF // 2), pl.ds(HALF // 2, HALF // 2)

    def piece(layer, part, to):
        return s0.at[layer, :, part, at_x(to)]

    def hop(layer, i):
        source = (
            lambda: piece(layer, low, far), lambda: piece(layer, high, far),
            lambda: piece(layer, high, right), lambda: piece(layer, low, left),
            lambda: sx.at[layer, 0], lambda: sx.at[layer, 1],
        )[i]()
        return pltpu.make_async_remote_copy(
            src_ref=source, dst_ref=rx.at[layer, i],
            send_sem=sem_x.at[0, layer, i], recv_sem=sem_x.at[1, layer, i],
            device_id=x_dev(left if i % 2 else right), device_id_type=pl.DeviceIdType.MESH,
        )

    def x_first(layer):
        for i in range(4):
            hop(layer, i).start()

    def x_merge(layer):
        for i, own in ((0, piece(layer, low, right)), (1, piece(layer, high, left))):
            hop(layer, i).wait_recv()
            sx[layer, i] = (own[...].astype(F32) + rx[layer, i].astype(F32)).astype(BF)
            hop(layer, 4 + i).start()

    def x_sum(layer):
        for i in (2, 3, 4, 5):
            hop(layer, i).wait_recv()
        for part, a, b in ((low, 3, 4), (high, 2, 5)):
            total = (
                piece(layer, part, x)[...].astype(F32) + rx[layer, a].astype(F32)
                + rx[layer, b].astype(F32)
            )
            sy[layer, :, part, :] = total.astype(BF)
        ex_y[layer].push()

    unit = lax.broadcasted_iota(jnp.int32, (C, C), 0) == lax.broadcasted_iota(jnp.int32, (C, C), 1)
    unit = unit.astype(F32).astype(BF)
    for load, w, wt in ((loads[0], w1, w1t), (loads[1], w2, w2t)):
        load.wait()
        for k in range(3):
            wt[k * C : (k + 1) * C, :] = nt(unit, w[k * C : (k + 1) * C, :]).astype(BF)

    forward(0)
    second_delta(0)
    terms(1, d2, hq, S2, lambda: None)
    first_delta(0)
    pair_sum(1)
    x_first(1)
    terms(0, d1, fq, S1, lambda: x_merge(1))
    pair_sum(0)
    x_first(0)
    x_sum(1)
    input_grad(0)
    x_merge(0)
    send_grad(0)

    def gather(ex, own, n, me):
        ex.dst(me)[...] = own
        ex.land()
        ref = ex.dst
        total = ref(0)[...].astype(F32)
        for t in range(1, n):
            total = total + ref(t)[...].astype(F32)
        return total

    x_sum(0)
    s2[3:6] = gather(ex_y[1], sy[1, :, at_y(y), :], NY, y).astype(BF)
    s2[0:3] = gather(ex_y[0], sy[0, :, at_y(y), :], NY, y).astype(BF)
    ex_z.push()
    grads[...] = gather(ex_z, s2[:, at_z(z), :], NZ, z)
    ex_g[0].land()

    for ex in (*ex_f, *ex_c, *ex_g, *ex_y, ex_z):
        ex.sent()
    for i in range(6):
        hop(0, i).wait_send()
        hop(1, i).wait_send()
    loop(0, 3, lambda k: swap(0, k).wait_send())
    loop(0, 3, lambda k: swap(1, k).wait_send())


def per_device(frames, cotangent, first_filter, second_filter):
    core = lax.axis_index("hosp") % NC
    zl = lax.axis_index("seq") // NX
    a = jnp.arange(C)
    width = C // NS
    i_from = ((a // width) % ZL) * (NX * width) + (a // (ZL * width)) * width + a % width
    perm_i = (a[:, None] == i_from[None, :]).astype(BF)
    owner = jnp.where(a < HALF, core, 1 - core)
    b = a % HALF
    o_from = ((b // ZW) % ZH) * (NY * NC * ZW) + (b // YW) * (NC * ZW) + owner * ZW + b % ZW
    perm_o = (o_from[:, None] == a[None, :]).astype(BF)

    vmem = pl.BlockSpec(memory_space=pltpu.VMEM)
    hbm = pl.BlockSpec(memory_space=pltpu.HBM)
    dma = pltpu.SemaphoreType.DMA
    out, grads = pl.pallas_call(
        kernel,
        out_shape=(
            jax.ShapeDtypeStruct((R, C), BF),
            jax.ShapeDtypeStruct((6, ZW, XW), F32),
        ),
        in_specs=[hbm] * 4 + [vmem] * 2,
        out_specs=(vmem, vmem),
        scratch_shapes=[
            pltpu.VMEM((PARTS, M + 2 * S1, C), BF),
            pltpu.VMEM((PARTS, M + 2 * S2, C), BF),
            pltpu.VMEM((PARTS, M + 2 * S1, C), BF),
            pltpu.VMEM((PARTS, M + 2 * S2, C), BF),
            pltpu.VMEM((PARTS, M + 2 * S1, C), BF),
            pltpu.VMEM((PARTS, M + 2 * S2, C), BF),
            pltpu.VMEM((PARTS, M, C), BF),
            pltpu.VMEM((PARTS, M, C), F32),
            pltpu.VMEM((PARTS, M, C), F32),
            pltpu.VMEM((PARTS, M, C), F32),
            pltpu.VMEM((PARTS, M, C), BF),
            pltpu.VMEM((C, M), BF),
            pltpu.VMEM((2, 3, HALF, C), F32),
            pltpu.VMEM((2, 3, HALF, C), BF),
            pltpu.VMEM((2, 3, HALF, C), BF),
            pltpu.VMEM((2, 3, HALF, C), BF),
            pltpu.VMEM((2, 2, 3, HALF // 2, XW), BF),
            pltpu.VMEM((2, 6, 3, HALF // 2, XW), BF),
            pltpu.VMEM((2, 3, HALF, XW), BF),
            pltpu.VMEM((2, NY, 3, YW, XW), BF),
            pltpu.VMEM((6, YW, XW), BF),
            pltpu.VMEM((NZ, 6, ZW, XW), BF),
            pltpu.VMEM((3 * C, C), BF),
            pltpu.VMEM((3 * C, C), BF),
            pltpu.VMEM((3 * C, C), BF),
            pltpu.VMEM((3 * C, C), BF),
            dma((8,)),
            dma((PARTS, 2, NS)),
            dma((PARTS, 2, NS)),
            dma((PARTS, 2, NS)),
            dma((2, 2, 3)),
            dma((2, 2, 6)),
            dma((2, 2, NY)),
            dma((2, NZ)),
        ],
        compiler_params=pltpu.CompilerParams(
            collective_id=0, has_side_effects=True, vmem_limit_bytes=56 * 1024 * 1024
        ),
    )(
        frames[0], cotangent[0],
        first_filter.reshape(3 * C, C), second_filter.reshape(3 * C, C),
        perm_i, perm_o,
    )
    scale = 1.0 / math.sqrt(lax.axis_size("hosp") * R * lax.axis_size("seq"))
    own = lax.dynamic_slice_in_dim(grads, zl * width, width, axis=2) * scale
    own = own.transpose(2, 0, 1)
    return (out[None], own[:, :3], own[:, 3:])


def solution(mesh):
    in_specs = (P("hosp", "seq", None), P("hosp", "seq", None), P(), P())
    out_specs = (P("hosp", "seq", None), P("seq", None, "hosp"), P("seq", None, "hosp"))
    return jax.shard_map(
        per_device, mesh=mesh, in_specs=in_specs, out_specs=out_specs, check_vma=False
    )
```

time: 87.1 us -> 83.3 us (0.956); the launches traced: 86.8 us -> 81.9 us
  local copies, waits for them, and re-layouts: 6.31 us -> 2.49 us
  Pallas kernels: 79.4 us -> 76.7 us
  other arithmetic: 0.39 us -> 2.03 us
    unnamed x9 -> x1, local copies, waits for them, and re-layouts: 5.69 us -> 1.87 us
    pallas_call x1, Pallas kernels: 79.4 us -> 76.7 us  [per_device(): pl.pallas_call(kernel, out_shape=(jax.ShapeDtypeStruct((R, C), BF), jax.S...]
where the time goes in v3:
time: 83.3 us; the launch traced here: 81.9 us
  Pallas kernels  76.7 us (92%)
  local copies, waits for them, and re-layouts  2.49 us (3%)
  other arithmetic  2.03 us (2%)
    pallas_call x1, Pallas kernels, per_device(): pl.pallas_call(kernel, out_shape=(jax.ShapeDtypeStruct((R, C), BF), jax.S...  76.7 us
    unnamed x1, local copies, waits for them, and re-layouts  1.87 us

profile of v3, /device:TPU:6, one launch (start us, length us, event | category | flops | bytes accessed | tf_op | source)
XLA Modules:
  0.0 81.9 jit_solution(8235937858897833569)
XLA Ops:
  0.7 1.1 %fusion = (bf16[512,512]{1,0:T(8,128)(2,1)}, bf16[512,512]{1,0:T(8,128)(2,1)}) fusion(s32[512]{0:T(512)S(1)} %fusion.9, s32[512]{0:T(512)S(1)} %fusion.15), kind=kLoop, calls=%fused_computation.2 | loop fusion | flops 1048576 | bytes 1052672 | tf_op jit(solution)/shard_map/convert_element_type | solution.py:354
  1.8 76.7 %shard_map.67 = (bf16[512,512]{1,0:T(8,128)(2,1)}, f32[6,16,128]{2,1,0:T(8,128)}) custom-call(bf16[512,512]{1,0:T(8,128)(2,1)} %bitcast.9, bf16[512,512]{1,0:T(8,128)(2,1)} %bitcast.10, bf16[1536,512]{1,0:T(8,128)(2,1)} %bitcast.7, bf16[1536,512]{1,0:T(8,128)(2,1)} %bitcast.8, bf16[512,512]{1,0:T(8,128)(2,1)} %get-tuple-element.9.perm_i, ...), custom_call_target="tpu_custom_call" | custom-call | tf_op jit(solution)/shard_map/pallas_call | solution.py:363
  78.5 0.9 %multiply_bitcast_fusion = f32[32,6,16]{0,2,1:T(8,128)S(1)} fusion(f32[6,16,128]{2,1,0:T(8,128)} %get-tuple-element.6, s32[]{:T(128)S(6)} %select_n.108), kind=kLoop, calls=%fused_computation.4 | loop fusion | flops 3072 | bytes 24580 | tf_op jit(solution)/shard_map/transpose | solution.py:417
  79.4 0.6 fusion.27
  80.0 1.9 %copy.8 = bf16[1,512,512]{2,1,0:T(8,128)(2,1)} copy(bf16[1,512,512]{2,1,0:T(8,128)(2,1)} %bitcast.11) | data formatting | bytes 1048576
  (2 shorter events, 0.0 us)

commit v4 on v3

--- a/solution.py
+++ b/solution.py
@@ -128,7 +128,11 @@
             )
 
         def push(self):
-            loop(1, self.n, lambda r: self.copy(r, lax.rem(self.me + r, self.n), self.me).start())
+            def body(r):
+                self.copy(r, lax.rem(self.me + r, self.n), self.me).start()
+
+            loop(self.n // 2, self.n, body)
+            loop(1, self.n // 2, body)
 
         def land(self):
             def body(r):

time: 83.3 us -> 81.7 us (0.981); the launches traced: 81.9 us -> 81.2 us
  no operation moved by 1% of the time
where the time goes in v4:
time: 81.7 us; the launch traced here: 81.2 us
  Pallas kernels  76 us (93%)
  local copies, waits for them, and re-layouts  2.49 us (3%)
  other arithmetic  2.03 us (2%)
    pallas_call x1, Pallas kernels, per_device(): pl.pallas_call(kernel, out_shape=(jax.ShapeDtypeStruct((R, C), BF), jax.S...  76 us
    unnamed x1, local copies, waits for them, and re-layouts  1.87 us

profile of v4, /device:TPU:6, one launch (start us, length us, event | category | flops | bytes accessed | tf_op | source)
XLA Modules:
  0.0 81.2 jit_solution(6647323950247370591)
XLA Ops:
  0.7 1.1 %fusion = (bf16[512,512]{1,0:T(8,128)(2,1)}, bf16[512,512]{1,0:T(8,128)(2,1)}) fusion(s32[512]{0:T(512)S(1)} %fusion.9, s32[512]{0:T(512)S(1)} %fusion.15), kind=kLoop, calls=%fused_computation.2 | loop fusion | flops 1048576 | bytes 1052672 | tf_op jit(solution)/shard_map/convert_element_type | solution.py:358
  1.8 76.0 %shard_map.67 = (bf16[512,512]{1,0:T(8,128)(2,1)}, f32[6,16,128]{2,1,0:T(8,128)}) custom-call(bf16[512,512]{1,0:T(8,128)(2,1)} %bitcast.9, bf16[512,512]{1,0:T(8,128)(2,1)} %bitcast.10, bf16[1536,512]{1,0:T(8,128)(2,1)} %bitcast.7, bf16[1536,512]{1,0:T(8,128)(2,1)} %bitcast.8, bf16[512,512]{1,0:T(8,128)(2,1)} %get-tuple-element.9.perm_i, ...), custom_call_target="tpu_custom_call" | custom-call | tf_op jit(solution)/shard_map/pallas_call | solution.py:367
  77.8 0.9 %multiply_bitcast_fusion = f32[32,6,16]{0,2,1:T(8,128)S(1)} fusion(f32[6,16,128]{2,1,0:T(8,128)} %get-tuple-element.6, s32[]{:T(128)S(6)} %select_n.108), kind=kLoop, calls=%fused_computation.4 | loop fusion | flops 3072 | bytes 24580 | tf_op jit(solution)/shard_map/transpose | solution.py:421
  78.7 0.6 fusion.27
  79.3 1.9 %copy.8 = bf16[1,512,512]{2,1,0:T(8,128)(2,1)} copy(bf16[1,512,512]{2,1,0:T(8,128)(2,1)} %bitcast.11) | data formatting | bytes 1048576
  (2 shorter events, 0.0 us)
